TPU v7x, 512 devices: a whole 4x4x16 slice. The times are simulated.
512 devices in a mesh: row: 16 (over x, y), col: 32 (over z, core).
Axes of the slice: x: 4, y: 4, z: 16, core: 2. Of those that a mesh axis runs over, the one named last changes fastest.
Arguments:
- l_rows: float32 [4096, 16384], P('row', 'col'), may hold values from -6 to 6
- v_prev: float32 [16384, 1024], P('col', 'row'), may hold values from -0.046875 to 0.046875
- l_tail: float32 [4096, 4096], P('row', 'col'), may hold values from -5 to 100, as said below
- k_cross: float32 [4096, 1024], P('row', 'col'), may hold values from -6 to 6
- k_query: float32 [1024, 1024], P('row', 'col'), may hold values from -2 to 5, as said below
Outputs:
- tail_solution: float32 [4096, 1024], P('row', 'col')
- posterior: float32 [1024, 1024], P('row', 'col')
Inputs may be any that keep to these rules, and one draw needn't show every extreme that they name: `l_tail`: lower triangular; its diagonal lies between 40 and 100. `k_query`: symmetric.
All inputs are finite; a program needn't handle non-finite values.
Results may differ from a plain program's by a relative error of at most 0.000076.
Values sent between devices are 32-bit elements; how exact they have to be, the bound alone decides.
No kernel may reach another device: no remote copies, remote signals or barrier semaphores. Data moves between devices by JAX's collectives and lax.ppermute only.
A program may use at most 64 MiB of HBM per device.

v0:
```python
import jax
import jax.numpy as jnp
from jax import lax
from jax.sharding import PartitionSpec as P


def spread(value, axis, root):
    mine = lax.axis_index(axis) == root
    return lax.psum(jnp.where(mine, value, jnp.zeros_like(value)), axis)


def body(l_rows, v_prev, l_tail, k_cross, k_query):
    highest = lax.Precision.HIGHEST
    tail_rows = l_rows.shape[0]
    shard_piece = lax.all_gather(v_prev, "row", axis=1, tiled=True)
    update = jnp.dot(l_rows, shard_piece, precision=highest, preferred_element_type=jnp.float32)
    own_gram = jnp.dot(v_prev.T, shard_piece, precision=highest, preferred_element_type=jnp.float32)
    partial_value = jnp.concatenate([update, own_gram], axis=0)
    summed = lax.psum_scatter(partial_value, "col", scatter_dimension=1, tiled=True)
    residual = k_cross - summed[:tail_rows]
    gram_prior = summed[tail_rows:]
    factor = lax.all_gather(l_tail, "col", axis=1, tiled=True)
    row_index = lax.axis_index("row")
    row_count = lax.axis_size("row")
    diagonal_block = lax.dynamic_slice_in_dim(factor, row_index * tail_rows, tail_rows, 1)
    query_cols = residual.shape[1]
    empty_block = jnp.zeros((tail_rows, query_cols), jnp.float32)

    def solve_block(right_side):
        return jax.scipy.linalg.solve_triangular(diagonal_block, right_side, lower=True)

    known_start = jnp.zeros((row_count * tail_rows, query_cols), jnp.float32)

    def advance(turn_index, carry):
        known_blocks, own_block = carry

        def compute_own():
            earlier = jnp.dot(
                factor, known_blocks, precision=highest, preferred_element_type=jnp.float32
            )
            return solve_block(residual - earlier)

        candidate = lax.cond(turn_index == row_index, compute_own, lambda: own_block)
        solved = spread(candidate, "row", turn_index)
        known_blocks = lax.dynamic_update_slice_in_dim(
            known_blocks, solved, turn_index * tail_rows, 0
        )
        own_block = jnp.where(turn_index == row_index, solved, own_block)
        return (known_blocks, own_block)

    known_blocks, own_block = lax.fori_loop(0, row_count, advance, (known_start, empty_block))
    cross_gram = jnp.dot(
        own_block.T,
        lax.all_gather(own_block, "col", axis=1, tiled=True),
        precision=highest,
        preferred_element_type=jnp.float32,
    )
    gram_tail = lax.psum_scatter(cross_gram, "row", scatter_dimension=1, tiled=True)
    posterior = k_query - gram_prior - gram_tail.T
    return (own_block, posterior)


def solution(mesh):
    in_specs = (P("row", "col"), P("col", "row"), P("row", "col"), P("row", "col"), P("row", "col"))
    out_specs = (P("row", "col"), P("row", "col"))
    return jax.shard_map(body, mesh=mesh, in_specs=in_specs, out_specs=out_specs, check_vma=False)
```

profile of v0, /device:TPU:6, one launch (start us, length us, event | category | flops | bytes accessed | tf_op | source)
XLA Modules:
  0.0 1905.1 jit_solution(9816575636633028090)
XLA Ops:
  8.0 67.4 %all-gather.6.cloned.1.call-done = f32[512,1024]{0,1:T(8,128)} async-done(((f32[512,64]{0,1:T(8,128)}), f32[512,1024]{0,1:T(8,128)}) %all-gather.6.cloned.1.call-update) | async-done | bytes 2097168 | tf_op jit(solution)/shard_map/all_gather | solution.py:15
  83.9 110.0 %reduce-scatter.7.cloned.1.call-done = f32[32,320]{1,0:T(8,128)} async-done(((f32[1024,320]{1,0:T(8,128)}), f32[32,320]{1,0:T(8,128)}) %reduce-scatter.7.cloned.1.call-update) | async-done | bytes 40976
  194.8 79.3 %all-gather.4.cloned.1.call-done = f32[256,4096]{1,0:T(8,128)} async-done(((f32[256,128]{1,0:T(8,128)}), f32[256,4096]{1,0:T(8,128)}) %all-gather.4.cloned.1.call-update) | async-done | bytes 4194320 | tf_op jit(solution)/shard_map/all_gather | solution.py:22
  275.2 1463.1 %while.21 = (s32[]{:T(128)}, f32[4096,32]{1,0:T(8,128)S(1)}, f32[256,32]{0,1:T(8,128)S(1)}, s32[]{:T(128)}, f32[256,256]{1,0:T(8,128)S(1)}, /*index=5*/f32[256,4...) while((s32[]{:T(128)}, f32[4096,32]{1,0:T(8,128)S(1)}, ...), condition=%wide.region_5.6_spmd.clone, body=%wide.region_1.5_spmd.clone.sunk | while | flops 421720064 | bytes 6439400 | solution.py:51
  275.3 92.3 %psum.13 = f32[256,32]{0,1:T(8,128)S(1)} all-reduce(f32[256,32]{0,1:T(8,128)S(1)} %broadcast_select_fusion.7), channel_id=1, replica_groups=mesh['row'=16,'col'=32] {'row'}, use_global_device_ids=true, to_apply=%region_4.4 | all-reduce | flops 8192 | bytes 65536 | tf_op jit(solution)/shard_map/while/body/eval_jaxpr/psum | solution.py:9
  367.8 97.9 %psum.13 = f32[256,32]{0,1:T(8,128)S(1)} all-reduce(f32[256,32]{0,1:T(8,128)S(1)} %broadcast_select_fusion.7), channel_id=1, replica_groups=mesh['row'=16,'col'=32] {'row'}, use_global_device_ids=true, to_apply=%region_4.4 | all-reduce | flops 8192 | bytes 65536 | tf_op jit(solution)/shard_map/while/body/eval_jaxpr/psum | solution.py:9
  465.9 92.9 %psum.13 = f32[256,32]{0,1:T(8,128)S(1)} all-reduce(f32[256,32]{0,1:T(8,128)S(1)} %broadcast_select_fusion.7), channel_id=1, replica_groups=mesh['row'=16,'col'=32] {'row'}, use_global_device_ids=true, to_apply=%region_4.4 | all-reduce | flops 8192 | bytes 65536 | tf_op jit(solution)/shard_map/while/body/eval_jaxpr/psum | solution.py:9
  559.0 91.3 %psum.13 = f32[256,32]{0,1:T(8,128)S(1)} all-reduce(f32[256,32]{0,1:T(8,128)S(1)} %broadcast_select_fusion.7), channel_id=1, replica_groups=mesh['row'=16,'col'=32] {'row'}, use_global_device_ids=true, to_apply=%region_4.4 | all-reduce | flops 8192 | bytes 65536 | tf_op jit(solution)/shard_map/while/body/eval_jaxpr/psum | solution.py:9
  650.5 88.7 %psum.13 = f32[256,32]{0,1:T(8,128)S(1)} all-reduce(f32[256,32]{0,1:T(8,128)S(1)} %broadcast_select_fusion.7), channel_id=1, replica_groups=mesh['row'=16,'col'=32] {'row'}, use_global_device_ids=true, to_apply=%region_4.4 | all-reduce | flops 8192 | bytes 65536 | tf_op jit(solution)/shard_map/while/body/eval_jaxpr/psum | solution.py:9
  739.4 89.4 %psum.13 = f32[256,32]{0,1:T(8,128)S(1)} all-reduce(f32[256,32]{0,1:T(8,128)S(1)} %broadcast_select_fusion.7), channel_id=1, replica_groups=mesh['row'=16,'col'=32] {'row'}, use_global_device_ids=true, to_apply=%region_4.4 | all-reduce | flops 8192 | bytes 65536 | tf_op jit(solution)/shard_map/while/body/eval_jaxpr/psum | solution.py:9
  829.0 85.6 %psum.13 = f32[256,32]{0,1:T(8,128)S(1)} all-reduce(f32[256,32]{0,1:T(8,128)S(1)} %broadcast_select_fusion.7), channel_id=1, replica_groups=mesh['row'=16,'col'=32] {'row'}, use_global_device_ids=true, to_apply=%region_4.4 | all-reduce | flops 8192 | bytes 65536 | tf_op jit(solution)/shard_map/while/body/eval_jaxpr/psum | solution.py:9
  914.9 89.5 %psum.13 = f32[256,32]{0,1:T(8,128)S(1)} all-reduce(f32[256,32]{0,1:T(8,128)S(1)} %broadcast_select_fusion.7), channel_id=1, replica_groups=mesh['row'=16,'col'=32] {'row'}, use_global_device_ids=true, to_apply=%region_4.4 | all-reduce | flops 8192 | bytes 65536 | tf_op jit(solution)/shard_map/while/body/eval_jaxpr/psum | solution.py:9
  1004.6 89.8 %psum.13 = f32[256,32]{0,1:T(8,128)S(1)} all-reduce(f32[256,32]{0,1:T(8,128)S(1)} %broadcast_select_fusion.7), channel_id=1, replica_groups=mesh['row'=16,'col'=32] {'row'}, use_global_device_ids=true, to_apply=%region_4.4 | all-reduce | flops 8192 | bytes 65536 | tf_op jit(solution)/shard_map/while/body/eval_jaxpr/psum | solution.py:9
  1094.7 91.6 %psum.13 = f32[256,32]{0,1:T(8,128)S(1)} all-reduce(f32[256,32]{0,1:T(8,128)S(1)} %broadcast_select_fusion.7), channel_id=1, replica_groups=mesh['row'=16,'col'=32] {'row'}, use_global_device_ids=true, to_apply=%region_4.4 | all-reduce | flops 8192 | bytes 65536 | tf_op jit(solution)/shard_map/while/body/eval_jaxpr/psum | solution.py:9
  1186.5 87.7 %psum.13 = f32[256,32]{0,1:T(8,128)S(1)} all-reduce(f32[256,32]{0,1:T(8,128)S(1)} %broadcast_select_fusion.7), channel_id=1, replica_groups=mesh['row'=16,'col'=32] {'row'}, use_global_device_ids=true, to_apply=%region_4.4 | all-reduce | flops 8192 | bytes 65536 | tf_op jit(solution)/shard_map/while/body/eval_jaxpr/psum | solution.py:9
  1274.5 89.6 %psum.13 = f32[256,32]{0,1:T(8,128)S(1)} all-reduce(f32[256,32]{0,1:T(8,128)S(1)} %broadcast_select_fusion.7), channel_id=1, replica_groups=mesh['row'=16,'col'=32] {'row'}, use_global_device_ids=true, to_apply=%region_4.4 | all-reduce | flops 8192 | bytes 65536 | tf_op jit(solution)/shard_map/while/body/eval_jaxpr/psum | solution.py:9
  1364.2 30.0 %conditional.3 = (f32[256,32]{0,1:T(8,128)S(1)}) conditional(s32[]{:T(128)} %convert_element_type.9, f32[256,32]{0,1:T(8,128)S(1)} %broadcast_select_fusion.6, (f32[256,256]{1,0:T(8,128)S(1)}, f32[256,4096]{1,0:T(8,128)}, f32[4096,32]{1,0:T(8,128)S(1)}, f32[256,32]{0,1:T(8,128)S(1)}) %tuple.65), branch_computations={%region_2.0_spmd, %region_3.3_spmd} | conditional | flops 421679104 | bytes 5816525 | solution.py:43
  1373.9 19.7 %custom-call.3 = f32[2,128,128]{1,2,0:T(8,128)S(1)} custom-call(f32[2,128,128]{2,1,0:T(8,128)S(1)} %get-tuple-element.154), custom_call_target="InvertDiagBlocksLowerTriangular" | custom-call | tf_op jit(solution)/shard_map/while/body/eval_jaxpr/cond/branch_1_fun/jit(_solve_triangular)/triangular_solve | solution.py:30
  1394.2 59.9 %psum.13 = f32[256,32]{0,1:T(8,128)S(1)} all-reduce(f32[256,32]{0,1:T(8,128)S(1)} %broadcast_select_fusion.7), channel_id=1, replica_groups=mesh['row'=16,'col'=32] {'row'}, use_global_device_ids=true, to_apply=%region_4.4 | all-reduce | flops 8192 | bytes 65536 | tf_op jit(solution)/shard_map/while/body/eval_jaxpr/psum | solution.py:9
  1454.3 91.4 %psum.13 = f32[256,32]{0,1:T(8,128)S(1)} all-reduce(f32[256,32]{0,1:T(8,128)S(1)} %broadcast_select_fusion.7), channel_id=1, replica_groups=mesh['row'=16,'col'=32] {'row'}, use_global_device_ids=true, to_apply=%region_4.4 | all-reduce | flops 8192 | bytes 65536 | tf_op jit(solution)/shard_map/while/body/eval_jaxpr/psum | solution.py:9
  1545.9 92.9 %psum.13 = f32[256,32]{0,1:T(8,128)S(1)} all-reduce(f32[256,32]{0,1:T(8,128)S(1)} %broadcast_select_fusion.7), channel_id=1, replica_groups=mesh['row'=16,'col'=32] {'row'}, use_global_device_ids=true, to_apply=%region_4.4 | all-reduce | flops 8192 | bytes 65536 | tf_op jit(solution)/shard_map/while/body/eval_jaxpr/psum | solution.py:9
  1639.0 99.1 %psum.13 = f32[256,32]{0,1:T(8,128)S(1)} all-reduce(f32[256,32]{0,1:T(8,128)S(1)} %broadcast_select_fusion.7), channel_id=1, replica_groups=mesh['row'=16,'col'=32] {'row'}, use_global_device_ids=true, to_apply=%region_4.4 | all-reduce | flops 8192 | bytes 65536 | tf_op jit(solution)/shard_map/while/body/eval_jaxpr/psum | solution.py:9
  1739.0 68.6 %all-gather.8.cloned.1.call-done = f32[256,1024]{0,1:T(8,128)} async-done(((f32[256,32]{0,1:T(8,128)}), f32[256,1024]{0,1:T(8,128)}) %all-gather.8.cloned.1.call-update) | async-done | bytes 1048592 | tf_op jit(solution)/shard_map/all_gather | solution.py:54
  1811.5 85.7 %reduce-scatter.9.cloned.1.call-done = f32[64,32]{1,0:T(8,128)} async-done(((f32[1024,32]{1,0:T(8,128)}), f32[64,32]{1,0:T(8,128)}) %reduce-scatter.9.cloned.1.call-update) | async-done | bytes 8208 | tf_op jit(solution)/shard_map/transpose | solution.py:59
  (149 shorter events, 33.8 us)
Async XLA Ops:
  7.2 72.1 %copy-start = (f32[256,512]{1,0:T(8,128)S(1)}, f32[256,512]{1,0:T(8,128)}, u32[]{:S(2)}) copy-start(f32[256,512]{1,0:T(8,128)} %param.9) | copy-start | bytes 1572868
  7.2 68.1 %all-gather.6.cloned.1.call-start = ((), (), s32[]{:S(2)}) async-start(), calls=%async_computation.3 | async-start | bytes 2228224 | tf_op jit(solution)/shard_map/all_gather | solution.py:15
  7.9 185.9 %reduce-scatter.7.cloned.1.call-start = ((), (), s32[]{:S(2)}) async-start(), calls=%async_computation.5 | async-start | bytes 1622016
  75.3 3.9 copy-start.1
  81.3 2.5 copy-start.3
  83.0 191.1 %all-gather.4.cloned.1.call-start = ((), (), s32[]{:S(2)}) async-start(), calls=%async_computation.2 | async-start | bytes 4325376 | tf_op jit(solution)/shard_map/all_gather | solution.py:22
  83.7 1723.8 %all-gather.8.cloned.1.call-start = ((), (), s32[]{:S(2)}) async-start(), calls=%async_computation.4 | async-start | bytes 1081344 | tf_op jit(solution)/shard_map/all_gather | solution.py:54
  1738.3 0.6 copy-start.2
  1738.3 72.3 %copy-start.4 = (f32[64,32]{0,1:T(8,128)S(1)}, f32[64,32]{0,1:T(8,128)}, u32[]{:S(2)}) copy-start(f32[64,32]{0,1:T(8,128)} %param.13) | copy-start | bytes 24580
  1739.0 158.2 %reduce-scatter.9.cloned.1.call-start = ((), (), s32[]{:S(2)}) async-start(), calls=%async_computation.6 | async-start | bytes 557056 | tf_op jit(solution)/shard_map/transpose | solution.py:59
Sparse Core Ops, SparseCore 0:
  11.0 64.2 all-gather.5
  83.1 110.7 reduce-scatter.6
  195.9 78.1 all-gather.3
  1739.1 68.4 all-gather.7
  1811.5 85.6 reduce-scatter.8
where the time goes:
time: 1910 us
  blocking collectives  1430 us (75%)
  waiting for transfers between devices  412 us (22%)
  other arithmetic  21 us (1%)
    psum x16, blocking collectives, spread(): return lax.psum(jnp.where(mine, value, jnp.zeros_like(value)), axis)  1430 us
    unnamed x6, waiting for transfers between devices  111 us
    transpose x1, waiting for transfers between devices, body(): posterior = k_query - gram_prior - gram_tail.T  85.7 us
    all_gather x1, waiting for transfers between devices, body(): factor = lax.all_gather(l_tail, 'col', axis=1, tiled=True)  79.3 us
    all_gather x1, waiting for transfers between devices, body(): lax.all_gather(own_block, 'col', axis=1, tiled=True)  68.6 us
    all_gather x1, waiting for transfers between devices, body(): shard_piece = lax.all_gather(v_prev, 'row', axis=1, tiled=True)  67.4 us
  transfers between devices with their start and end apart: 5, of which 5 were waited for; matrix products, arithmetic and copies ran while one was open for 0% of the time, Pallas kernels for 0%

commit v1 on v0

v1 whole, which is shorter than its diff:
```python
import functools
import jax
import jax.numpy as jnp
from jax import lax
from jax.experimental import pallas as pl
from jax.experimental.pallas import tpu as pltpu
from jax.sharding import Mesh, PartitionSpec as P

HI = lax.Precision.HIGHEST
PLANE = ("x", "y")
PLANE_T = ("y", "x")


def contract(a, b, dims):
    return lax.dot_general(a, b, (dims, ((), ())), precision=HI, preferred_element_type=jnp.float32)


def share(value, axis, count):
    return lax.all_to_all(jnp.broadcast_to(value[None], (count,) + value.shape), axis, 0, 0)


def swap(value):
    return lax.ppermute(value, "k", [(0, 1), (1, 0)])


def invert_kernel(d_ref, o_ref):
    d = d_ref[...]
    n = d.shape[0]
    row = lax.broadcasted_iota(jnp.int32, (n, n), 0)
    col = lax.broadcasted_iota(jnp.int32, (n, n), 1)
    x = jnp.where(row == col, 1.0 / d, 0.0)
    b = 1
    while b < n:
        same = (row // (2 * b)) == (col // (2 * b))
        below = same & ((row // b) % 2 == 1) & ((col // b) % 2 == 0)
        off = jnp.where(below, d, 0.0)
        t = jnp.dot(x, off, precision=HI, preferred_element_type=jnp.float32)
        x = x - jnp.dot(t, x, precision=HI, preferred_element_type=jnp.float32)
        b *= 2
    o_ref[...] = x


def invert(d):
    return pl.pallas_call(
        invert_kernel,
        out_shape=jax.ShapeDtypeStruct(d.shape, jnp.float32),
        in_specs=[pl.BlockSpec(memory_space=pltpu.VMEM)],
        out_specs=pl.BlockSpec(memory_space=pltpu.VMEM),
        name="invert_block",
    )(d)


def body(l_rows, v_prev, l_tail, k_cross, k_query):
    x_id, y_id, k_id = lax.axis_index("x"), lax.axis_index("y"), lax.axis_index("k")
    rows = l_rows.shape[0]
    qc = k_cross.shape[1]

    with jax.named_scope("gather_l"):
        panels = lax.all_gather(l_tail, ("zh", "zl", "k"), axis=0)

    with jax.named_scope("stage1"):
        vt = v_prev.T
        vt_other = swap(vt)
        l_other = swap(l_rows)
        v_pair = jnp.concatenate([vt, vt_other], axis=1)
        l_pair = jnp.concatenate([l_rows, l_other], axis=1)
        v_half = lax.dynamic_slice_in_dim(v_pair, k_id * qc, qc, 0)
        v_all = share(v_half, PLANE_T, 16)
        update = contract(v_all, l_pair, ((2,), (1,)))
        prior = contract(v_all, v_pair, ((2,), (1,)))
    with jax.named_scope("reduce_z"):
        both = jnp.concatenate([update, prior], axis=2).reshape(4, 4, qc, -1)
        both = lax.all_to_all(both, "zl", 0, 0).sum(0)
        both = lax.all_to_all(both, "zh", 0, 0).sum(0)
        rest = k_cross.T - both[:, :rows]
        gram_prior = both[:, rows:]

    with jax.named_scope("inverse"):
        factor = panels.transpose(1, 0, 2).reshape(rows, -1)
        own = lax.dynamic_slice_in_dim(factor, x_id * 4 * rows, 4 * rows, 1)
        diag = invert(lax.dynamic_slice_in_dim(own, y_id * rows, rows, 1))
        sent = jnp.concatenate([own[:, : 3 * rows], diag], axis=1)
        group = share(sent, "y", 4)
        zero = jnp.zeros_like(diag)
        inv = [None] * 4
        for m in (3, 2, 1, 0):
            if m < 3:
                left = jnp.concatenate(inv[m + 1 :], axis=1)
                right = group[m + 1 :, :, m * rows : (m + 1) * rows].reshape(-1, rows)
                t = contract(left, right, ((1,), (0,)))
                t = contract(t, group[m, :, 3 * rows :], ((1,), (0,)))
                inv[m] = jnp.where(m == y_id, diag, jnp.where(m < y_id, -t, zero))
            else:
                inv[m] = jnp.where(m == y_id, diag, zero)
        inverse = jnp.concatenate(inv, axis=1)

    solved = jnp.zeros_like(rest)
    for j in range(4):
        with jax.named_scope(f"solve{j}"):
            right = share(rest, "y", 4).transpose(1, 0, 2).reshape(qc, -1)
            mine = contract(right, inverse, ((1,), (1,)))
            solved = jnp.where(x_id == j, mine, solved)
            if j < 3:
                known = share(solved, PLANE, 16)[4 * j : 4 * j + 4]
                known = known.transpose(1, 0, 2).reshape(qc, -1)
                rest = rest - contract(known, factor[:, j * 4 * rows : (j + 1) * 4 * rows], ((1,), (1,)))

    with jax.named_scope("gram"):
        near = share(solved, "zh", 4)
        near = share(near, "zl", 4)
        far = swap(near)
        ga = contract(near, solved, ((3,), (1,)))
        gb = contract(far, solved, ((3,), (1,)))
        first = jnp.where(k_id == 0, ga, gb)
        second = jnp.where(k_id == 0, gb, ga)
        part = jnp.concatenate([first, second], axis=2).reshape(16, 2 * qc, qc)
        gram_tail = lax.all_to_all(part, PLANE_T, 0, 0).sum(0)
        posterior = k_query - (gram_prior.T + gram_tail)
    return solved.T, posterior


def solution(mesh):
    fine = Mesh(mesh.devices.reshape(4, 4, 4, 4, 2), ("x", "y", "zh", "zl", "k"))
    row, col = ("x", "y"), ("zh", "zl", "k")
    in_specs = (P(row, col), P(col, row), P(row, col), P(row, col), P(row, col))
    return jax.shard_map(body, mesh=fine, in_specs=in_specs, out_specs=(P(row, col), P(row, col)), check_vma=False)
```

time: 1910 us -> 346 us (0.18)
  blocking collectives: 1430 us -> 111 us
  waiting for transfers between devices: 412 us -> 112 us
  starting transfers between devices: 0.2 us -> 45.8 us
    psum x16 -> x0, blocking collectives: 1430 us -> none  [spread(): return lax.psum(jnp.where(mine, value, jnp.zeros_like(value)), axis)]
    all_gather x3 -> x1, waiting for transfers between devices: 215 us -> 0.01 us  [body(): panels = lax.all_gather(l_tail, ('zh', 'zl', 'k'), axis=0)]
    all_to_all x0 -> x7, blocking collectives: none -> 111 us  [the longest x5 71.1 us: share(): lax.all_to_all(jnp.broadcast_to(value[None], (count,) + value.shape), axi...]
    unnamed x6 -> x1, waiting for transfers between devices: 111 us -> 0.68 us
    all_to_all x0 -> x7, waiting for transfers between devices: none -> 109 us  [the longest x6 93.9 us: share(): lax.all_to_all(jnp.broadcast_to(value[None], (count,) + value.shape), axi...]
    transpose x1 -> x0, waiting for transfers between devices: 85.7 us -> none  [body(): posterior = k_query - gram_prior - gram_tail.T]
    all_to_all x0 -> x7, starting transfers between devices: none -> 39.7 us  [the longest x6 28.8 us: share(): lax.all_to_all(jnp.broadcast_to(value[None], (count,) + value.shape), axi...]
    another operation x4 -> x0, other arithmetic: 19.7 us -> none  [solve_block(): jax.scipy.linalg.solve_triangular(diagonal_block, right_side, lower=True)]
  transfers between devices with their start and end apart: 5 -> 11, of which waited for: 5 -> 8; matrix products, arithmetic and copies ran while one was open for 0% -> 6% of each run, Pallas kernels for 0% -> 3%
where the time goes in v1:
time: 346 us; the launch traced here: 342 us
  waiting for transfers between devices  112 us (32%)
  blocking collectives  111 us (32%)
  starting transfers between devices  45.8 us (13%)
  matrix products  23.8 us (7%)
  local copies, waits for them, and re-layouts  21.4 us (6%)
  between operations  14.6 us (4%)
  Pallas kernels  9.5 us (3%)
  other arithmetic  4.47 us (1%)
    all_to_all x6, waiting for transfers between devices, share(): lax.all_to_all(jnp.broadcast_to(value[None], (count,) + value.shape), axi...  93.9 us
    all_to_all x5, blocking collectives, share(): lax.all_to_all(jnp.broadcast_to(value[None], (count,) + value.shape), axi...  71.1 us
    all_to_all x1, blocking collectives, body(): both = lax.all_to_all(both, 'zl', 0, 0).sum(0)  29.5 us
    all_to_all x6, starting transfers between devices, share(): lax.all_to_all(jnp.broadcast_to(value[None], (count,) + value.shape), axi...  28.8 us
    dot_general x17, matrix products, contract(): lax.dot_general(a, b, (dims, ((), ())), precision=HI, preferred_element_t...  23.8 us
    all_to_all x1, waiting for transfers between devices, body(): both = lax.all_to_all(both, 'zh', 0, 0).sum(0)  15.3 us
    all_to_all x1, starting transfers between devices, body(): both = lax.all_to_all(both, 'zh', 0, 0).sum(0)  11 us
    all_to_all x1, blocking collectives, body(): gram_tail = lax.all_to_all(part, PLANE_T, 0, 0).sum(0)  10.7 us
  transfers between devices with their start and end apart: 11, of which 8 were waited for; matrix products, arithmetic and copies ran while one was open for 6% of the time, Pallas kernels for 3%

profile of v1, /device:TPU:6, one launch (start us, length us, event | category | flops | bytes accessed | tf_op | source)
XLA Modules:
  0.0 342.4 jit_solution(6559291118950110817)
XLA Ops:
  13.8 9.3 %all-to-all-start = ((f32[16,32,1024]{2,1,0:T(8,128)}), f32[16,32,1024]{2,1,0:T(8,128)S(1)}, u32[]{:S(2)}, u32[]{:S(2)}) async-start(f32[16,32,1024]{2,1,0:T(8,128)} %broadcast_in_dim.26), calls=%async_computation | async-start | bytes 4194304 | tf_op jit(solution)/shard_map/stage1/all_to_all | solution.py:19
  25.1 29.0 %all-to-all-done = f32[16,32,1024]{2,1,0:T(8,128)S(1)} async-done(((f32[16,32,1024]{2,1,0:T(8,128)}), f32[16,32,1024]{2,1,0:T(8,128)S(1)}, u32[]{:S(2)}, u32[]{:S(2)}) %all-to-all-start) | async-done | bytes 2097184 | tf_op jit(solution)/shard_map/stage1/all_to_all | solution.py:19
  57.9 29.5 %all_to_all.70 = f32[4,4,32,320]{3,2,1,0:T(8,128)S(1)} all-to-all(f32[4,4,32,320]{3,2,1,0:T(8,128)S(1)} %bitcast.99), channel_id=1, replica_groups=mesh['x'=4,'y'=4,'zh'=4,'zl'=4,'k'=2] {'zl'}, dimensions={0} | all-to-all | bytes 1310720 | tf_op jit(solution)/shard_map/reduce_z/all_to_all | solution.py:73
  88.0 11.0 %all-to-all-start.2 = ((f32[4,32,320]{2,1,0:T(8,128)}), f32[4,32,320]{2,1,0:T(8,128)S(1)}, u32[]{:S(2)}, u32[]{:S(2)}) async-start(f32[4,32,320]{2,1,0:T(8,128)} %reduce_sum.27), calls=%async_computation.2 | async-start | bytes 393216 | tf_op jit(solution)/shard_map/reduce_z/all_to_all | solution.py:74
  99.0 15.3 %all-to-all-done.2 = f32[4,32,320]{2,1,0:T(8,128)S(1)} async-done(((f32[4,32,320]{2,1,0:T(8,128)}), f32[4,32,320]{2,1,0:T(8,128)S(1)}, u32[]{:S(2)}, u32[]{:S(2)}) %all-to-all-start.2) | async-done | bytes 163872 | tf_op jit(solution)/shard_map/reduce_z/all_to_all | solution.py:74
  115.0 4.5 %all-to-all-start.3 = ((f32[4,32,256]{2,1,0:T(8,128)}), f32[4,32,256]{2,1,0:T(8,128)S(1)}, u32[]{:S(2)}, u32[]{:S(2)}) async-start(f32[4,32,256]{2,1,0:T(8,128)} %broadcast_in_dim.27), calls=%async_computation.3 | async-start | bytes 262144 | tf_op jit(solution)/shard_map/solve0/all_to_all | solution.py:19
  119.5 4.6 %copy.27 = f32[32,256,128]{2,0,1:T(8,128)S(1)} copy(f32[32,256,128]{2,1,0:T(8,128)} %bitcast.97) | data formatting | bytes 8388608 | tf_op jit(solution)/shard_map/gather_l/all_gather | solution.py:59
  124.1 3.8 %copy.50 = f32[32,8,32,128]{3,1,2,0:T(8,128)S(1)} copy(f32[32,8,32,128]{3,2,1,0:T(8,128)S(1)} %bitcast.96) | data formatting | bytes 8388608
  130.7 9.5 %invert_block.1 = f32[256,256]{1,0:T(8,128)} custom-call(f32[256,256]{1,0:T(8,128)} %constant_dynamic-slice_fusion.1.d_ref), custom_call_target="tpu_custom_call" | custom-call | tf_op jit(solution)/shard_map/inverse/invert_block/pallas_call | solution.py:44
  141.3 2.5 broadcast_in_dim.29
  143.8 5.0 %all-to-all-start.4 = ((f32[4,256,1024]{2,1,0:T(8,128)}), f32[4,256,1024]{2,1,0:T(8,128)}, u32[]{:S(2)}, u32[]{:S(2)}) async-start(f32[4,256,1024]{2,1,0:T(8,128)} %broadcast_in_dim.29), calls=%async_computation.4 | async-start | bytes 8388608 | tf_op jit(solution)/shard_map/inverse/all_to_all | solution.py:19
  148.8 44.5 %all-to-all-done.4 = f32[4,256,1024]{2,1,0:T(8,128)} async-done(((f32[4,256,1024]{2,1,0:T(8,128)}), f32[4,256,1024]{2,1,0:T(8,128)}, u32[]{:S(2)}, u32[]{:S(2)}) %all-to-all-start.4) | async-done | bytes 4194336 | tf_op jit(solution)/shard_map/inverse/all_to_all | solution.py:19
  203.5 13.2 %all_to_all.71 = f32[16,32,256]{2,1,0:T(8,128)S(1)} all-to-all(f32[16,32,256]{2,1,0:T(8,128)S(1)} %broadcast_in_dim.31), channel_id=1, replica_groups=mesh['x'=4,'y'=4,'zh'=4,'zl'=4,'k'=2] {'x','y'}, dimensions={0} | all-to-all | bytes 1048576 | tf_op jit(solution)/shard_map/solve0/all_to_all | solution.py:19
  219.7 3.3 all-to-all-start.6
  223.0 5.9 %all-to-all-done.6 = f32[4,32,256]{2,1,0:T(8,128)S(1)} async-done(((f32[4,32,256]{2,1,0:T(8,128)}), f32[4,32,256]{2,1,0:T(8,128)S(1)}, u32[]{:S(2)}, u32[]{:S(2)}) %all-to-all-start.6) | async-done | bytes 131104 | tf_op jit(solution)/shard_map/solve1/all_to_all | solution.py:19
  230.0 13.0 %all_to_all.72 = f32[16,32,256]{2,1,0:T(8,128)S(1)} all-to-all(f32[16,32,256]{2,1,0:T(8,128)S(1)} %broadcast_in_dim.33), channel_id=1, replica_groups=mesh['x'=4,'y'=4,'zh'=4,'zl'=4,'k'=2] {'x','y'}, dimensions={0} | all-to-all | bytes 1048576 | tf_op jit(solution)/shard_map/solve1/all_to_all | solution.py:19
  246.0 3.3 all-to-all-start.8
  249.3 8.5 %all-to-all-done.8 = f32[4,32,256]{2,1,0:T(8,128)S(1)} async-done(((f32[4,32,256]{2,1,0:T(8,128)}), f32[4,32,256]{2,1,0:T(8,128)S(1)}, u32[]{:S(2)}, u32[]{:S(2)}) %all-to-all-start.8) | async-done | bytes 131104 | tf_op jit(solution)/shard_map/solve2/all_to_all | solution.py:19
  258.9 13.2 %all_to_all.73 = f32[16,32,256]{2,1,0:T(8,128)S(1)} all-to-all(f32[16,32,256]{2,1,0:T(8,128)S(1)} %broadcast_in_dim.35), channel_id=1, replica_groups=mesh['x'=4,'y'=4,'zh'=4,'zl'=4,'k'=2] {'x','y'}, dimensions={0} | all-to-all | bytes 1048576 | tf_op jit(solution)/shard_map/solve2/all_to_all | solution.py:19
  275.0 3.3 all-to-all-start.10
  278.4 5.9 %all-to-all-done.10 = f32[4,32,256]{2,1,0:T(8,128)S(1)} async-done(((f32[4,32,256]{2,1,0:T(8,128)}), f32[4,32,256]{2,1,0:T(8,128)S(1)}, u32[]{:S(2)}, u32[]{:S(2)}) %all-to-all-start.10) | async-done | bytes 131104 | tf_op jit(solution)/shard_map/solve3/all_to_all | solution.py:19
  285.4 17.3 %all_to_all.74 = f32[4,32,256]{2,1,0:T(8,128)S(1)} all-to-all(f32[4,32,256]{2,1,0:T(8,128)S(1)} %broadcast_in_dim.37), channel_id=1, replica_groups=mesh['x'=4,'y'=4,'zh'=4,'zl'=4,'k'=2] {'zh'}, dimensions={0} | all-to-all | bytes 262144 | tf_op jit(solution)/shard_map/gram/all_to_all | solution.py:19
  302.7 14.5 %all_to_all.75 = f32[4,4,32,256]{3,2,1,0:T(8,128)S(1)} all-to-all(f32[4,4,32,256]{3,2,1,0:T(8,128)S(1)} %broadcast_in_dim.38), channel_id=1, replica_groups=mesh['x'=4,'y'=4,'zh'=4,'zl'=4,'k'=2] {'zl'}, dimensions={0} | all-to-all | bytes 1048576 | tf_op jit(solution)/shard_map/gram/all_to_all | solution.py:19
  322.6 10.7 %all_to_all.76 = f32[16,1,2048]{2,1,0:T(1,128)S(1)} all-to-all(f32[16,1,2048]{2,1,0:T(1,128)S(1)} %reshape.71), channel_id=1, replica_groups=mesh['x'=4,'y'=4,'zh'=4,'zl'=4,'k'=2] {'y','x'}, dimensions={0} | all-to-all | bytes 262144 | tf_op jit(solution)/shard_map/gram/all_to_all | solution.py:117
  (79 shorter events, 47.3 us)
Async XLA Ops:
  7.2 47.0 %copy-start.3 = (f32[512,64]{0,1:T(8,128)S(1)}, f32[512,64]{0,1:T(8,128)}, u32[]{:S(2)}) copy-start(f32[512,64]{0,1:T(8,128)} %param.6) | copy-start | bytes 393220
  7.2 16.0 %copy-start.2 = (f32[256,512]{1,0:T(8,128)S(1)}, f32[256,512]{1,0:T(8,128)}, u32[]{:S(2)}) copy-start(f32[256,512]{1,0:T(8,128)} %param.5) | copy-start | bytes 1572868
  7.2 112.3 %all-gather.3.cloned.1.call-start = ((), (), s32[]{:S(2)}) async-start(), calls=%async_computation.14 | async-start | bytes 4325376 | tf_op jit(solution)/shard_map/gather_l/all_gather | solution.py:59
  7.9 3.5 %collective-permute-start = (f32[64,512]{1,0:T(8,128)}, f32[64,512]{1,0:T(8,128)S(1)}, u32[]{:S(2)}, u32[]{:S(2)}) collective-permute-start(f32[64,512]{1,0:T(8,128)} %bitcast.102), channel_id=1, source_target_pairs={{0,1},{1,0},{2,3},{3,2},{4,5},{5,4},{6,7},{7,6},{8,9},{9,8},{10,11... | collective-permute-start | bytes 393224 | tf_op jit(solution)/shard_map/stage1/ppermute | solution.py:23
  13.8 40.3 %all-to-all-start = ((f32[16,32,1024]{2,1,0:T(8,128)}), f32[16,32,1024]{2,1,0:T(8,128)S(1)}, u32[]{:S(2)}, u32[]{:S(2)}) async-start(f32[16,32,1024]{2,1,0:T(8,128)} %broadcast_in_dim.26), calls=%async_computation | async-start | bytes 4194304 | tf_op jit(solution)/shard_map/stage1/all_to_all | solution.py:19
  23.2 32.7 %collective-permute-start.1 = (f32[256,512]{1,0:T(8,128)S(1)}, f32[256,512]{1,0:T(8,128)S(1)}, u32[]{:S(2)}, u32[]{:S(2)}) collective-permute-start(f32[256,512]{1,0:T(8,128)S(1)} %copy-done.2), channel_id=1, source_target_pairs={{0,1},{1,0},{2,3},{3,2},{4,5},{5,4},{6,7},{7,6},{8,9},{9,8},{10,11... | collective-permute-start | bytes 1572872 | tf_op jit(solution)/shard_map/stage1/ppermute | solution.py:23
  55.9 58.4 %copy-start.5 = (f32[256,32]{0,1:T(8,128)S(1)}, f32[256,32]{0,1:T(8,128)}, u32[]{:S(2)}) copy-start(f32[256,32]{0,1:T(8,128)} %param.8) | copy-start | bytes 98308
  88.0 26.2 %all-to-all-start.2 = ((f32[4,32,320]{2,1,0:T(8,128)}), f32[4,32,320]{2,1,0:T(8,128)S(1)}, u32[]{:S(2)}, u32[]{:S(2)}) async-start(f32[4,32,320]{2,1,0:T(8,128)} %reduce_sum.27), calls=%async_computation.2 | async-start | bytes 393216 | tf_op jit(solution)/shard_map/reduce_z/all_to_all | solution.py:74
  115.0 26.3 %all-to-all-start.3 = ((f32[4,32,256]{2,1,0:T(8,128)}), f32[4,32,256]{2,1,0:T(8,128)S(1)}, u32[]{:S(2)}, u32[]{:S(2)}) async-start(f32[4,32,256]{2,1,0:T(8,128)} %broadcast_in_dim.27), calls=%async_computation.3 | async-start | bytes 262144 | tf_op jit(solution)/shard_map/solve0/all_to_all | solution.py:19
  127.9 2.0 copy-start
  143.8 5.0 %copy-start.1 = (f32[256,256]{1,0:T(8,128)S(1)}, f32[256,256]{1,0:T(8,128)}, u32[]{:S(2)}) copy-start(f32[256,256]{1,0:T(8,128)} %invert_block.1) | copy-start | bytes 786436
  143.8 49.6 %all-to-all-start.4 = ((f32[4,256,1024]{2,1,0:T(8,128)}), f32[4,256,1024]{2,1,0:T(8,128)}, u32[]{:S(2)}, u32[]{:S(2)}) async-start(f32[4,256,1024]{2,1,0:T(8,128)} %broadcast_in_dim.29), calls=%async_computation.4 | async-start | bytes 8388608 | tf_op jit(solution)/shard_map/inverse/all_to_all | solution.py:19
  219.7 9.3 %all-to-all-start.6 = ((f32[4,32,256]{2,1,0:T(8,128)}), f32[4,32,256]{2,1,0:T(8,128)S(1)}, u32[]{:S(2)}, u32[]{:S(2)}) async-start(f32[4,32,256]{2,1,0:T(8,128)} %broadcast_in_dim.32), calls=%async_computation.6 | async-start | bytes 262144 | tf_op jit(solution)/shard_map/solve1/all_to_all | solution.py:19
  246.0 11.8 %all-to-all-start.8 = ((f32[4,32,256]{2,1,0:T(8,128)}), f32[4,32,256]{2,1,0:T(8,128)S(1)}, u32[]{:S(2)}, u32[]{:S(2)}) async-start(f32[4,32,256]{2,1,0:T(8,128)} %broadcast_in_dim.34), calls=%async_computation.8 | async-start | bytes 262144 | tf_op jit(solution)/shard_map/solve2/all_to_all | solution.py:19
  275.0 9.3 %all-to-all-start.10 = ((f32[4,32,256]{2,1,0:T(8,128)}), f32[4,32,256]{2,1,0:T(8,128)S(1)}, u32[]{:S(2)}, u32[]{:S(2)}) async-start(f32[4,32,256]{2,1,0:T(8,128)} %broadcast_in_dim.36), calls=%async_computation.10 | async-start | bytes 262144 | tf_op jit(solution)/shard_map/solve3/all_to_all | solution.py:19
  284.3 50.6 %copy-start.6 = (f32[64,32]{0,1:T(8,128)S(1)}, f32[64,32]{0,1:T(8,128)}, u32[]{:S(2)}) copy-start(f32[64,32]{0,1:T(8,128)} %param.9) | copy-start | bytes 24580
  285.4 50.2 %copy-start.4 = (f32[32,256]{1,0:T(8,128)}, f32[32,256]{1,0:T(8,128)S(1)}, u32[]{:S(2)}) copy-start(f32[32,256]{1,0:T(8,128)S(1)} %convolution_select_fusion) | copy-start | bytes 98308
  317.2 3.8 %collective-permute-start.2 = (f32[4,4,32,256]{3,2,1,0:T(8,128)S(1)}, f32[4,4,32,256]{3,2,1,0:T(8,128)S(1)}, u32[]{:S(2)}, u32[]{:S(2)}) collective-permute-start(f32[4,4,32,256]{3,2,1,0:T(8,128)S(1)} %all_to_all.75), channel_id=1, source_target_pairs={{0,1},{1,0},{2,3},{3,2},{4,5},{5,4},{6,7},{7,6},{8,9},{9,8},{10,11... | collective-permute-start | bytes 1572872 | tf_op jit(solution)/shard_map/gram/ppermute | solution.py:23
Sparse Core Ops, SparseCore 0:
  10.1 85.0 all-gather.2
